TPU v7x, 32 devices: a whole 2x2x4 slice. The times are simulated.
32 devices in a mesh: shot: 2 (over y), row: 4 (over x, core), freq: 4 (over z).
Axes of the slice: x: 2, y: 2, z: 4, core: 2. Of those that a mesh axis runs over, the one named last changes fastest.
Arguments:
- source_field: float32 [2, 8, 1024, 1024], P(None, ('shot', 'freq'), 'row'), parts along dimension 1, may hold values from -6 to 6
- receiver_field: float32 [2, 8, 1024, 1024], P(None, ('shot', 'freq'), 'row'), parts along dimension 1, may hold values from -6 to 6
- slowness: float32 [4, 1024, 1024], P('freq', 'row'), may hold values from 0.22 to 0.67
- owner: int32 [4], replicated, may hold values from 0 to 3, each once
- freq_index: int32 [8], P(('shot', 'freq')), parts along dimension 0, may hold values from 0 to 3, each once
Outputs:
- source_out: float32 [2, 8, 1024, 1024], P(None, ('shot', 'freq'), 'row'), parts along dimension 1
- receiver_out: float32 [2, 8, 1024, 1024], P(None, ('shot', 'freq'), 'row'), parts along dimension 1
- image: float32 [4, 1024, 1024], P('shot', 'row', 'freq'), parts along dimension 0
There are 2 independent parts, one for each index of `shot`. A program takes and returns all parts, laid end to end along the dimension named above; an argument that names none is the same for every part. Nothing has to cross between parts.
All inputs are finite; a program needn't handle non-finite values.
Results may differ from a plain program's by a relative error of at most 0.00022.
Values sent between devices are 32-bit elements; how exact they have to be, the bound alone decides.
A program may use at most 128 MiB of HBM per device.

v0:
```python
import math
import jax
import jax.numpy as jnp
from jax import lax
from jax.sharding import PartitionSpec as P

NZ = 2
dz_km = 0.01
dx_km = 0.0125
ref_slow = 0.5
base_hertz = 3.0
step_hertz = 4.0
taper = 0.5


def spread(value, axis, source):
    kept = jnp.where(lax.axis_index(axis) == source, value, 0).astype(value.dtype)
    return lax.psum(kept, axis)


def split_length(length):
    return length // 128


def angle_table(count_a, count_b, modulus, sign):
    left = jnp.arange(count_a, dtype=jnp.int32)[:, None]
    right = jnp.arange(count_b, dtype=jnp.int32)[None, :]
    turns = (left * right % modulus).astype(jnp.float32) * (2.0 * math.pi / modulus)
    return (jnp.cos(turns), sign * jnp.sin(turns))


def contract(form, left, right):
    return jnp.einsum(form, left, right, precision=lax.Precision.HIGHEST)


def transform_pair(real_part, imag_part, sign, last):
    length = real_part.shape[2] if last else real_part.shape[1]
    first = split_length(length)
    second = length // first
    cos_a, sin_a = angle_table(first, first, first, sign)
    cos_b, sin_b = angle_table(second, second, second, sign)
    twist_c, twist_s = angle_table(first, second, length, sign)
    if last:
        shape = (real_part.shape[0], real_part.shape[1], first, second)
        form_one = "fajb,jk->fakb"
        form_two = "fakb,bm->famk"
    else:
        shape = (real_part.shape[0], first, second, real_part.shape[2])
        form_one = "fjbq,jk->fkbq"
        form_two = "fkbq,bm->fmkq"
        twist_c = twist_c[:, :, None]
        twist_s = twist_s[:, :, None]
    x_re = real_part.reshape(shape)
    x_im = imag_part.reshape(shape)
    y_re = contract(form_one, x_re, cos_a) - contract(form_one, x_im, sin_a)
    y_im = contract(form_one, x_im, cos_a) + contract(form_one, x_re, sin_a)
    z_re = y_re * twist_c - y_im * twist_s
    z_im = y_im * twist_c + y_re * twist_s
    out_re = contract(form_two, z_re, cos_b) - contract(form_two, z_im, sin_b)
    out_im = contract(form_two, z_im, cos_b) + contract(form_two, z_re, sin_b)
    return (out_re.reshape(real_part.shape), out_im.reshape(real_part.shape))


def transform(block, sign, last):
    count = block.shape[0]
    freqs = block.shape[2]
    plane = block.shape[3:]
    real_part = block[:, 0].reshape((count * freqs,) + plane)
    imag_part = block[:, 1].reshape((count * freqs,) + plane)
    out_re, out_im = transform_pair(real_part, imag_part, sign, last)
    shape = (count, freqs) + plane
    return jnp.stack([out_re.reshape(shape), out_im.reshape(shape)], axis=1)


def wavenumbers(length, start, count):
    index = start + jnp.arange(count, dtype=jnp.int32)
    signed = jnp.where(index * 2 < length, index, index - length)
    return signed.astype(jnp.float32) * (2.0 * math.pi / (length * dx_km))


def rotate(block, cos_v, sin_v):
    real_part = block[:, 0]
    imag_part = block[:, 1]
    return jnp.stack(
        [real_part * cos_v - imag_part * sin_v, imag_part * cos_v + real_part * sin_v], axis=1
    )


def shift_phase(block, omega, kx_part, ky_part, total):
    square = kx_part[:, None] ** 2 + ky_part[None, :] ** 2
    kmax = math.pi / dx_km
    damp = jnp.exp(-taper * square / (kmax * kmax)) / total
    ws0 = omega[:, None, None] * ref_slow
    vertical = ws0 - 0.5 * square[None] / ws0
    cos_v = jnp.cos(dz_km * vertical) * damp
    sin_v = jnp.sin(dz_km * vertical) * damp
    return rotate(block, cos_v, sin_v)


def correct(block, slab, omega):
    theta = omega[:, None, None] * (slab[None] - ref_slow) * dz_km
    return rotate(block, jnp.cos(theta), jnp.sin(theta))


def image_term(block):
    return jnp.sum(block[0, 0] * block[1, 0] - block[0, 1] * block[1, 1], axis=0)


def body(source_field, receiver_field, slowness, owner, freq_index):
    rows = source_field.shape[2]
    width = source_field.shape[3]
    row_count = lax.axis_size("row")
    height = rows * row_count
    cols = width // row_count
    place = lax.axis_index("row")
    omega = 2.0 * math.pi * (base_hertz + step_hertz * freq_index.astype(jnp.float32))
    mirrored = jnp.stack([receiver_field[0], -receiver_field[1]])
    fields = jnp.stack([source_field, mirrored])
    kx_all = wavenumbers(height, 0, height)
    ky_own = wavenumbers(width, place * cols, cols)
    total = float(height * width)
    slab_dev = slowness.shape[0]
    images = []
    for depth in range(NZ):
        chosen = owner[depth]
        held = spread(slowness, "freq", chosen // slab_dev)
        slab = lax.dynamic_index_in_dim(held, chosen % slab_dev, 0, keepdims=False)
        fields = transform(fields, -1.0, True)
        fields = lax.all_to_all(fields, "row", split_axis=4, concat_axis=3, tiled=True)
        items = fields
        items = transform(items, -1.0, False)
        items = shift_phase(items, omega, kx_all, ky_own, total)
        fields = transform(items, 1.0, False)
        fields = lax.all_to_all(fields, "row", split_axis=3, concat_axis=4, tiled=True)
        fields = transform(fields, 1.0, True)
        fields = correct(fields, slab, omega)
        images.append(image_term(fields))
    parts = [lax.psum_scatter(term, "freq", scatter_dimension=1, tiled=True) for term in images]
    image = jnp.stack(parts)
    source_out = fields[0]
    receiver_out = jnp.stack([fields[1, 0], -fields[1, 1]])
    return (source_out, receiver_out, image)


def solution(mesh):
    in_specs = (
        P(None, ("shot", "freq"), "row", None),
        P(None, ("shot", "freq"), "row", None),
        P("freq", "row", None),
        P(),
        P(("shot", "freq")),
    )
    out_specs = (
        P(None, ("shot", "freq"), "row", None),
        P(None, ("shot", "freq"), "row", None),
        P("shot", "row", "freq"),
    )
    return jax.shard_map(body, mesh=mesh, in_specs=in_specs, out_specs=out_specs, check_vma=False)
```

profile of v0, /device:TPU:0, one launch (start us, length us, event | category | flops | bytes accessed | tf_op | source)
XLA Modules:
  0.0 596.2 jit_solution(643073891319918496)
XLA Ops:
  32.7 5.4 copy.346
  38.1 4.9 all-to-all-start
  48.1 43.7 %all-to-all-done = f32[2,2,1,256,1024]{3,0,2,1,4:T(2,128)} async-done(((f32[2,2,1,256,1024]{3,0,2,1,4:T(2,128)}), f32[2,2,1,256,1024]{3,0,2,1,4:T(2,128)}, u32[]{:S(2)}, u32[]{:S(2)}) %all-to-all-start) | async-done | bytes 4194336 | tf_op jit(solution)/shard_map/all_to_all | solution.py:129
  91.8 5.0 copy.347
  96.7 5.4 copy.348
  157.1 5.2 copy.372
  162.4 5.0 all-to-all-start.1
  171.0 90.0 %all-reduce.3.cloned.1.call-done = (f32[1,256,1024]{2,1,0:T(8,128)}, f32[1,256,1024]{2,1,0:T(8,128)}) async-done(((f32[1,256,1024]{2,1,0:T(8,128)}, f32[1,256,1024]{2,1,0:T(8,128)}), (f32[1,256,1024]{2,1,0:T(8,128)}, f32[1,256,1024]{2,1,0:T(8,128)})) %all-reduce.3.cloned.1.call-update) | async-done | bytes 2097168 | tf_op jit(solution)/shard_map/psum | solution.py:18
  260.9 4.7 fusion.192
  268.6 5.0 copy.373
  273.6 5.3 copy.374
  278.9 4.6 fusion.663
  315.4 4.8 fusion.314
  346.8 50.7 %all_to_all.72 = f32[2,2,1,256,1024]{3,0,2,1,4:T(2,128)S(1)} all-to-all(f32[2,2,1,256,1024]{3,0,2,1,4:T(2,128)S(1)} %copy.395), channel_id=1, replica_groups=mesh['shot'=2,'row'=4,'freq'=4] {'row'}, dimensions={4} | all-to-all | bytes 8388608 | tf_op jit(solution)/shard_map/all_to_all | solution.py:129
  400.3 5.7 copy.397
  460.8 5.2 copy.418
  466.0 4.9 all-to-all-start.3
  474.9 5.7 cosine_bitcast_fusion
  484.7 4.7 fusion.10
  490.7 28.5 %all-to-all-done.3 = f32[2,2,1,1024,256]{4,0,2,1,3:T(2,128)} async-done(((f32[2,2,1,1024,256]{4,0,2,1,3:T(2,128)}), f32[2,2,1,1024,256]{4,0,2,1,3:T(2,128)}, u32[]{:S(2)}, u32[]{:S(2)}) %all-to-all-start.3) | async-done | bytes 4194336 | tf_op jit(solution)/shard_map/all_to_all | solution.py:134
  519.2 5.0 copy.419
  524.2 5.3 copy.420
  529.4 4.6 fusion.661
  574.3 13.1 %reduce-scatter.5.cloned.1.call-done = f32[256,256]{0,1:T(8,128)} async-done(((f32[256,1024]{0,1:T(8,128)}), f32[256,256]{0,1:T(8,128)}) %reduce-scatter.5.cloned.1.call-update) | async-done | bytes 262160 | tf_op jit(solution)/shard_map/reduce_scatter | solution.py:138
  (177 shorter events, 256.6 us)
Async XLA Ops:
  8.9 1.6 copy-start.19
  38.1 53.7 %all-to-all-start = ((f32[2,2,1,256,1024]{3,0,2,1,4:T(2,128)}), f32[2,2,1,256,1024]{3,0,2,1,4:T(2,128)}, u32[]{:S(2)}, u32[]{:S(2)}) async-start(f32[2,2,1,256,1024]{3,0,2,1,4:T(2,128)} %copy.346), calls=%async_computation | async-start | bytes 8388608 | tf_op jit(solution)/shard_map/all_to_all | solution.py:129
  48.1 82.2 %copy-start.8 = (f32[8,128,256]{2,1,0:T(8,128)}, f32[8,128,256]{2,1,0:T(8,128)S(1)}, u32[]{:S(2)}) copy-start(f32[8,128,256]{2,1,0:T(8,128)S(1)} %get-tuple-element.67) | copy-start | bytes 3145732
  162.4 5.1 copy-start.21
  162.4 7.0 %copy-start.20 = (f32[1,256,1024]{2,1,0:T(8,128)S(1)}, f32[1,256,1024]{2,1,0:T(8,128)}, u32[]{:S(2)}) copy-start(f32[1,256,1024]{2,1,0:T(8,128)} %param.7) | copy-start | bytes 3145732
  162.4 106.2 %all-to-all-start.1 = ((f32[2,2,1,1024,256]{4,0,2,1,3:T(2,128)}), f32[2,2,1,1024,256]{4,0,2,1,3:T(2,128)}, u32[]{:S(2)}, u32[]{:S(2)}) async-start(f32[2,2,1,1024,256]{4,0,2,1,3:T(2,128)} %copy.372), calls=%async_computation.1 | async-start | bytes 8388608 | tf_op jit(solution)/shard_map/all_to_all | solution.py:134
  167.4 93.5 %all-reduce.3.cloned.1.call-start = ((), (), s32[]{:S(2)}) async-start(), calls=%async_computation.8 | async-start | bytes 4194304 | tf_op jit(solution)/shard_map/psum | solution.py:18
  265.7 2.9 copy-start.11
  265.7 2.9 copy-start.13
  285.6 3.2 copy-start.6
  291.1 1.9 copy-start.14
  293.0 2.0 copy-start.7
  323.2 3.6 copy-start.2
  323.3 3.6 copy-start.15
  326.9 2.0 copy-start.5
  466.0 53.1 %all-to-all-start.3 = ((f32[2,2,1,1024,256]{4,0,2,1,3:T(2,128)}), f32[2,2,1,1024,256]{4,0,2,1,3:T(2,128)}, u32[]{:S(2)}, u32[]{:S(2)}) async-start(f32[2,2,1,1024,256]{4,0,2,1,3:T(2,128)} %copy.418), calls=%async_computation.3 | async-start | bytes 8388608 | tf_op jit(solution)/shard_map/all_to_all | solution.py:134
  470.9 2.7 copy-start.12
  470.9 103.4 %reduce-scatter.3.cloned.1.call-start = ((), (), s32[]{:S(2)}) async-start(), calls=%async_computation.6 | async-start | bytes 1310720 | tf_op jit(solution)/shard_map/reduce_scatter | solution.py:138
  490.7 96.8 %reduce-scatter.5.cloned.1.call-start = ((), (), s32[]{:S(2)}) async-start(), calls=%async_computation.7 | async-start | bytes 1310720 | tf_op jit(solution)/shard_map/reduce_scatter | solution.py:138
  536.1 3.2 copy-start.3
  541.8 1.9 copy-start.16
  543.7 2.0 copy-start.4
  555.2 2.3 copy-start.10
  557.5 2.5 copy-start
  (4 other events, 5.3 us)
Sparse Core Ops, SparseCore 0:
  171.2 89.6 all-reduce.2
  490.8 26.5 reduce-scatter.2
  562.2 25.1 reduce-scatter.4
where the time goes:
time: 606 us; the launch traced here: 596 us
  waiting for transfers between devices  175 us (29%)
  matrix products  170 us (28%)
  local copies, waits for them, and re-layouts  125 us (21%)
  blocking collectives  50.7 us (8%)
  other arithmetic  42.9 us (7%)
  between operations  17.4 us (3%)
  starting transfers between devices  14.9 us (2%)
    dot_general x64, matrix products, contract(): return jnp.einsum(form, left, right, precision=lax.Precision.HIGHEST)  170 us
    psum x1, waiting for transfers between devices, spread(): return lax.psum(kept, axis)  90 us
    all_to_all x1, blocking collectives, body(): lax.all_to_all(fields, 'row', split_axis=4, concat_axis=3, tiled=True)  50.7 us
    all_to_all x1, waiting for transfers between devices, body(): lax.all_to_all(fields, 'row', split_axis=4, concat_axis=3, tiled=True)  43.7 us
    all_to_all x2, waiting for transfers between devices, body(): lax.all_to_all(fields, 'row', split_axis=3, concat_axis=4, tiled=True)  28.5 us
    all_to_all x4, local copies, waits for them, and re-layouts, body(): lax.all_to_all(fields, 'row', split_axis=3, concat_axis=4, tiled=True)  20.5 us
    another operation x4, local copies, waits for them, and re-layouts, transform(): return jnp.stack([out_re.reshape(shape), out_im.reshape(shape)], axis=1)  19.1 us
    all_to_all x4, local copies, waits for them, and re-layouts, body(): lax.all_to_all(fields, 'row', split_axis=4, concat_axis=3, tiled=True)  18.9 us
  transfers between devices with their start and end apart: 6, of which 4 were waited for; matrix products, arithmetic and copies ran while one was open for 15% of the time, Pallas kernels for 0%

commit v1 on v0

--- a/solution.py
+++ b/solution.py
@@ -11,6 +11,22 @@
 base_hertz = 3.0
 step_hertz = 4.0
 taper = 0.5
+
+
+def swapped_with_each(array, axis, split, join):
+    ways, here = (lax.axis_size(axis), lax.axis_index(axis))
+    width = array.shape[split] // ways
+    shape = list(array.shape)
+    shape[split] = width
+    height = shape[join]
+    shape[join] = height * ways
+    full = jnp.zeros(shape, array.dtype)
+    for mask in range(ways):
+        part = lax.dynamic_slice_in_dim(array, (here ^ mask) * width, width, axis=split)
+        if mask:
+            part = lax.ppermute(part, axis, [(d, d ^ mask) for d in range(ways)])
+        full = lax.dynamic_update_slice_in_dim(full, part, (here ^ mask) * height, axis=join)
+    return full
 
 
 def spread(value, axis, source):
@@ -131,7 +147,7 @@
         items = transform(items, -1.0, False)
         items = shift_phase(items, omega, kx_all, ky_own, total)
         fields = transform(items, 1.0, False)
-        fields = lax.all_to_all(fields, "row", split_axis=3, concat_axis=4, tiled=True)
+        fields = swapped_with_each(fields, "row", 3, 4)
         fields = transform(fields, 1.0, True)
         fields = correct(fields, slab, omega)
         images.append(image_term(fields))

time: 606 us -> 514 us (0.85)
  waiting for transfers between devices: 175 us -> 112 us
  local copies, waits for them, and re-layouts: 125 us -> 103 us
    psum x1, waiting for transfers between devices: 90 us -> 0.01 us  [spread(): return lax.psum(kept, axis)]
    ppermute x0 -> x6, waiting for transfers between devices: none -> 56.3 us  [swapped_with_each(): part = lax.ppermute(part, axis, [(d, d ^ mask) for d in range(ways)])]
    all_to_all x2 -> x0, waiting for transfers between devices: 28.5 us -> none  [body(): lax.all_to_all(fields, 'row', split_axis=3, concat_axis=4, tiled=True)]
    all_to_all x4 -> x0, local copies, waits for them, and re-layouts: 20.5 us -> none  [body(): lax.all_to_all(fields, 'row', split_axis=3, concat_axis=4, tiled=True)]
    dynamic_update_slice x0 -> x6, local copies, waits for them, and re-layouts: none -> 14.2 us  [swapped_with_each(): lax.dynamic_update_slice_in_dim(full, part, (here ^ mask) * height, axis=...]
    another operation x4 -> x2, local copies, waits for them, and re-layouts: 19.1 us -> 8.67 us  [transform(): return jnp.stack([out_re.reshape(shape), out_im.reshape(shape)], axis=1)]
    all_to_all x2 -> x0, starting transfers between devices: 9.89 us -> none  [body(): lax.all_to_all(fields, 'row', split_axis=3, concat_axis=4, tiled=True)]
    slice x2 -> x0, local copies, waits for them, and re-layouts: 9.2 us -> none  [transform(): imag_part = block[:, 1].reshape((count * freqs,) + plane)]
  transfers between devices with their start and end apart: 6 -> 10, of which waited for: 4 -> 6; matrix products, arithmetic and copies ran while one was open for 15% -> 30% of each run, Pallas kernels for 0% -> 0%
where the time goes in v1:
time: 514 us; the launch traced here: 505 us
  matrix products  167 us (32%)
  waiting for transfers between devices  112 us (22%)
  local copies, waits for them, and re-layouts  103 us (20%)
  blocking collectives  50.7 us (10%)
  other arithmetic  45.6 us (9%)
  between operations  17.6 us (3%)
  starting transfers between devices  9.04 us (2%)
    dot_general x64, matrix products, contract(): return jnp.einsum(form, left, right, precision=lax.Precision.HIGHEST)  167 us
    ppermute x6, waiting for transfers between devices, swapped_with_each(): part = lax.ppermute(part, axis, [(d, d ^ mask) for d in range(ways)])  56.3 us
    all_to_all x1, blocking collectives, body(): lax.all_to_all(fields, 'row', split_axis=4, concat_axis=3, tiled=True)  50.7 us
    all_to_all x1, waiting for transfers between devices, body(): lax.all_to_all(fields, 'row', split_axis=4, concat_axis=3, tiled=True)  40.1 us
    all_to_all x4, local copies, waits for them, and re-layouts, body(): lax.all_to_all(fields, 'row', split_axis=4, concat_axis=3, tiled=True)  19.1 us
    reduce_scatter x2, waiting for transfers between devices, body(): lax.psum_scatter(term, 'freq', scatter_dimension=1, tiled=True)  15.8 us
    dynamic_update_slice x6, local copies, waits for them, and re-layouts, swapped_with_each(): lax.dynamic_update_slice_in_dim(full, part, (here ^ mask) * height, axis=...  14.2 us
    sub x5, other arithmetic, rotate(): real_part * cos_v - imag_part * sin_v  13 us
  transfers between devices with their start and end apart: 10, of which 6 were waited for; matrix products, arithmetic and copies ran while one was open for 30% of the time, Pallas kernels for 0%

profile of v1, /device:TPU:0, one launch (start us, length us, event | category | flops | bytes accessed | tf_op | source)
XLA Modules:
  0.0 504.8 jit_solution(6449799745272319637)
XLA Ops:
  32.4 5.4 %copy.234 = f32[2,2,1,256,1024]{3,0,2,1,4:T(2,128)} copy(f32[2,2,1,256,1024]{3,4,0,2,1:T(8,128)S(1)} %pad_maximum_fusion) | data formatting | bytes 8388608 | tf_op jit(solution)/shard_map/stack | solution.py:88
  37.8 5.0 all-to-all-start
  47.4 4.0 fusion.214
  51.5 40.1 %all-to-all-done = f32[2,2,1,256,1024]{3,0,2,1,4:T(2,128)} async-done(((f32[2,2,1,256,1024]{3,0,2,1,4:T(2,128)}), f32[2,2,1,256,1024]{3,0,2,1,4:T(2,128)}, u32[]{:S(2)}, u32[]{:S(2)}) %all-to-all-start) | async-done | bytes 4194336 | tf_op jit(solution)/shard_map/all_to_all | solution.py:145
  91.6 5.0 copy.235
  96.6 5.7 %copy.236 = f32[2,2,1,4,256,256]{5,4,3,1,0,2:T(8,128)} copy(f32[2,2,1,4,256,256]{4,5,3,1,0,2:T(8,128)} %bitcast.509) | data formatting | bytes 8388608 | tf_op jit(solution)/shard_map/all_to_all | solution.py:145
  113.6 3.6 subtract_bitcast_fusion.13
  139.8 4.0 subtract_bitcast_fusion.11
  163.4 4.7 fusion.230
  173.4 14.4 %collective-permute-done.1 = f32[2,2,1,256,256]{4,3,0,2,1:T(8,128)} collective-permute-done((f32[2,2,1,256,256]{4,3,0,2,1:T(8,128)}, f32[2,2,1,256,256]{4,3,0,2,1:T(8,128)}, u32[]{:S(2)}, u32[]{:S(2)}) %collective-permute-start.1) | collective-permute-done | bytes 1048608 | tf_op jit(solution)/shard_map/ppermute | solution.py:27
  190.2 19.3 %collective-permute-done.2 = f32[2,2,1,256,256]{4,3,0,2,1:T(8,128)} collective-permute-done((f32[2,2,1,256,256]{4,3,0,2,1:T(8,128)}, f32[2,2,1,256,256]{4,3,0,2,1:T(8,128)}, u32[]{:S(2)}, u32[]{:S(2)}) %collective-permute-start.2) | collective-permute-done | bytes 1048608 | tf_op jit(solution)/shard_map/ppermute | solution.py:27
  241.5 4.8 fusion.382
  249.4 3.6 fusion.384
  269.7 3.2 copy.278
  272.9 50.7 %all_to_all.36 = f32[2,2,1,256,1024]{3,0,2,1,4:T(2,128)S(1)} all-to-all(f32[2,2,1,256,1024]{3,0,2,1,4:T(2,128)S(1)} %copy.278), channel_id=1, replica_groups=mesh['shot'=2,'row'=4,'freq'=4] {'row'}, dimensions={4} | all-to-all | bytes 8388608 | tf_op jit(solution)/shard_map/all_to_all | solution.py:145
  326.4 5.6 %copy.280 = f32[2,2,1,4,256,256]{5,4,3,1,0,2:T(8,128)} copy(f32[2,2,1,4,256,256]{4,5,3,1,0,2:T(8,128)} %bitcast.510) | data formatting | bytes 8388608 | tf_op jit(solution)/shard_map/all_to_all | solution.py:145
  343.2 3.6 subtract_bitcast_fusion.5
  369.4 3.9 subtract_bitcast_fusion.3
  391.5 4.6 cosine_bitcast_fusion
  405.6 4.7 fusion.26
  414.1 3.3 collective-permute-done.4
  419.8 19.3 %collective-permute-done.5 = f32[2,2,1,256,256]{4,3,0,2,1:T(8,128)} collective-permute-done((f32[2,2,1,256,256]{4,3,0,2,1:T(8,128)}, f32[2,2,1,256,256]{4,3,0,2,1:T(8,128)}, u32[]{:S(2)}, u32[]{:S(2)}) %collective-permute-start.5) | collective-permute-done | bytes 1048608 | tf_op jit(solution)/shard_map/ppermute | solution.py:27
  473.4 4.5 fusion.30
  479.8 15.8 %reduce-scatter.5.cloned.1.call-done = f32[256,256]{0,1:T(8,128)} async-done(((f32[256,1024]{0,1:T(8,128)}), f32[256,256]{0,1:T(8,128)}) %reduce-scatter.5.cloned.1.call-update) | async-done | bytes 262160 | tf_op jit(solution)/shard_map/reduce_scatter | solution.py:154
  (177 shorter events, 248.1 us)
Async XLA Ops:
  9.0 1.6 copy-start.13
  37.8 5.0 %copy-start.16 = (s32[4]{0:T(128)S(1)}, s32[4]{0:T(128)}, u32[]{:S(2)}) copy-start(s32[4]{0:T(128)} %param.8) | copy-start | bytes 52
  37.8 6.9 %copy-start.14 = (f32[1,256,1024]{2,1,0:T(8,128)S(1)}, f32[1,256,1024]{2,1,0:T(8,128)}, u32[]{:S(2)}) copy-start(f32[1,256,1024]{2,1,0:T(8,128)} %param.7) | copy-start | bytes 3145732
  37.8 53.8 %all-to-all-start = ((f32[2,2,1,256,1024]{3,0,2,1,4:T(2,128)}), f32[2,2,1,256,1024]{3,0,2,1,4:T(2,128)}, u32[]{:S(2)}, u32[]{:S(2)}) async-start(f32[2,2,1,256,1024]{3,0,2,1,4:T(2,128)} %copy.234), calls=%async_computation | async-start | bytes 8388608 | tf_op jit(solution)/shard_map/all_to_all | solution.py:145
  42.8 120.6 %all-reduce.3.cloned.1.call-start = ((), (), s32[]{:S(2)}) async-start(), calls=%async_computation.6 | async-start | bytes 4194304 | tf_op jit(solution)/shard_map/psum | solution.py:34
  46.3 433.5 %reduce-scatter.3.cloned.1.call-start = ((), (), s32[]{:S(2)}) async-start(), calls=%async_computation.4 | async-start | bytes 1310720 | tf_op jit(solution)/shard_map/reduce_scatter | solution.py:154
  51.5 78.8 %copy-start.4 = (f32[8,128,256]{2,1,0:T(8,128)}, f32[8,128,256]{2,1,0:T(8,128)S(1)}, u32[]{:S(2)}) copy-start(f32[8,128,256]{2,1,0:T(8,128)S(1)} %get-tuple-element.72) | copy-start | bytes 3145732
  161.6 9.5 %collective-permute-start = (f32[2,2,1,256,256]{4,3,0,2,1:T(8,128)}, f32[2,2,1,256,256]{4,3,0,2,1:T(8,128)}, u32[]{:S(2)}, u32[]{:S(2)}) collective-permute-start(f32[2,2,1,256,256]{4,3,0,2,1:T(8,128)} %get-tuple-element.54), channel_id=1, source_target_pairs={{0,4},{4,0},{8,12},{12,8},{1,5},{5,1},{9,13},{13,9},{2,6},{6,2},{1... | collective-permute-start | bytes 3145736 | tf_op jit(solution)/shard_map/ppermute | solution.py:27
  161.6 26.3 %collective-permute-start.1 = (f32[2,2,1,256,256]{4,3,0,2,1:T(8,128)}, f32[2,2,1,256,256]{4,3,0,2,1:T(8,128)}, u32[]{:S(2)}, u32[]{:S(2)}) collective-permute-start(f32[2,2,1,256,256]{4,3,0,2,1:T(8,128)} %get-tuple-element.55), channel_id=1, source_target_pairs={{0,8},{4,12},{8,0},{12,4},{1,9},{5,13},{9,1},{13,5},{2,10},{6,14},... | collective-permute-start | bytes 3145736 | tf_op jit(solution)/shard_map/ppermute | solution.py:27
  161.6 48.0 %collective-permute-start.2 = (f32[2,2,1,256,256]{4,3,0,2,1:T(8,128)}, f32[2,2,1,256,256]{4,3,0,2,1:T(8,128)}, u32[]{:S(2)}, u32[]{:S(2)}) collective-permute-start(f32[2,2,1,256,256]{4,3,0,2,1:T(8,128)} %get-tuple-element.52), channel_id=1, source_target_pairs={{0,12},{4,8},{8,4},{12,0},{1,13},{5,9},{9,5},{13,1},{2,14},{6,10},... | collective-permute-start | bytes 3145736 | tf_op jit(solution)/shard_map/ppermute | solution.py:27
  168.2 2.9 copy-start.7
  168.2 2.9 copy-start.9
  234.5 1.5 copy-start.12
  249.4 3.6 copy-start.2
  249.4 3.6 copy-start.10
  253.0 2.0 copy-start.3
  389.0 2.5 copy-start.15
  391.1 20.6 %collective-permute-start.3 = (f32[2,2,1,256,256]{4,3,0,2,1:T(8,128)}, f32[2,2,1,256,256]{4,3,0,2,1:T(8,128)}, u32[]{:S(2)}, u32[]{:S(2)}) collective-permute-start(f32[2,2,1,256,256]{4,3,0,2,1:T(8,128)} %get-tuple-element.46), channel_id=1, source_target_pairs={{0,4},{4,0},{8,12},{12,8},{1,5},{5,1},{9,13},{13,9},{2,6},{6,2},{1... | collective-permute-start | bytes 3145736 | tf_op jit(solution)/shard_map/ppermute | solution.py:27
  391.1 26.3 %collective-permute-start.4 = (f32[2,2,1,256,256]{4,3,0,2,1:T(8,128)}, f32[2,2,1,256,256]{4,3,0,2,1:T(8,128)}, u32[]{:S(2)}, u32[]{:S(2)}) collective-permute-start(f32[2,2,1,256,256]{4,3,0,2,1:T(8,128)} %get-tuple-element.47), channel_id=1, source_target_pairs={{0,8},{4,12},{8,0},{12,4},{1,9},{5,13},{9,1},{13,5},{2,10},{6,14},... | collective-permute-start | bytes 3145736 | tf_op jit(solution)/shard_map/ppermute | solution.py:27
  391.5 7.1 %copy-start.8 = (f32[1,256,1024]{2,1,0:T(8,128)S(1)}, f32[1,256,1024]{2,1,0:T(8,128)}, u32[]{:S(2)}) copy-start(f32[1,256,1024]{2,1,0:T(8,128)} %copy-done.7) | copy-start | bytes 3145732
  404.1 35.0 %collective-permute-start.5 = (f32[2,2,1,256,256]{4,3,0,2,1:T(8,128)}, f32[2,2,1,256,256]{4,3,0,2,1:T(8,128)}, u32[]{:S(2)}, u32[]{:S(2)}) collective-permute-start(f32[2,2,1,256,256]{4,3,0,2,1:T(8,128)} %get-tuple-element.44), channel_id=1, source_target_pairs={{0,12},{4,8},{8,4},{12,0},{1,13},{5,9},{9,5},{13,1},{2,14},{6,10},... | collective-permute-start | bytes 3145736 | tf_op jit(solution)/shard_map/ppermute | solution.py:27
  411.5 84.2 %reduce-scatter.5.cloned.1.call-start = ((), (), s32[]{:S(2)}) async-start(), calls=%async_computation.5 | async-start | bytes 1310720 | tf_op jit(solution)/shard_map/reduce_scatter | solution.py:154
  460.3 2.4 copy-start.6
  462.7 2.5 copy-start
  (3 other events, 3.8 us)
Sparse Core Ops, SparseCore 0:
  46.6 90.1 all-reduce.2
  411.6 28.3 reduce-scatter.2
  467.3 28.2 reduce-scatter.4
